TPU v7x, 128 devices: a whole 4x4x4 slice. The times are simulated.
128 devices in a mesh: member: 8 (over z, core), band: 16 (over x, y).
Axes of the slice: x: 4, y: 4, z: 4, core: 2. Of those that a mesh axis runs over, the one named last changes fastest.
Arguments:
- latent: bfloat16 [8, 4096, 1024], P('member', 'band'), may hold values from -6 to 6
- observed: bfloat16 [4096, 128], P('band'), may hold values from -6 to 6
- area_weight: float32 [4096], P('band'), may hold values from 0.3 to 25, as said below
- band_counts: int32 [16], replicated, may hold values from 128 to 256, as said below
- gain_attn: float32 [1024], replicated, may hold values from 0.25 to 1.75
- w_query: bfloat16 [1024, 1024], replicated, may hold values from -0.1875 to 0.1875
- w_key: bfloat16 [1024, 1024], replicated, may hold values from -0.1875 to 0.1875
- w_value: bfloat16 [1024, 1024], replicated, may hold values from -0.1875 to 0.1875
- w_out: bfloat16 [1024, 1024], replicated, may hold values from -1.5 to 1.5
- gain_head: float32 [1024], replicated, may hold values from 0.25 to 1.75
- w_head: bfloat16 [1024, 128], replicated, may hold values from -0.1875 to 0.1875
Outputs:
- grad_latent: bfloat16 [8, 4096, 1024], P('member', 'band')
- grad_head: float32 [1024, 128], P('band')
- ensemble_loss: float32 [], replicated
Inputs may be any that keep to these rules, and one draw needn't show every extreme that they name: Band b holds band_counts[b] live grid points in its first slots; the remaining of its 256 slots are padding. In every draw some band holds exactly 256 and another exactly 128. `area_weight`: positive area weights.
All inputs are finite; a program needn't handle non-finite values.
Results may differ from a plain program's by a relative error of at most 0.019.
Values may be sent and summed in bfloat16 or wider, within the bound.
No kernel may reach another device: no remote copies, remote signals or barrier semaphores. Data moves between devices by JAX's collectives and lax.ppermute only.
A program may use at most 192 MiB of HBM per device.

v0:
```python
import math
import jax
import jax.numpy as jnp
from jax import lax
from jax.sharding import PartitionSpec as P

HEADS = 16
CH = 128
R = 512
HOPS = 4
NORM_EPS = 1e-06
SMOOTH_WIDTH = 0.25
FAIR_ALPHA = 0.95
heads_per_group = 4


def from_behind(value, axis, steps):
    count = lax.axis_size(axis)
    leading, last = (max(0, -steps), min(count, count - steps))
    return lax.ppermute(value, axis, [(source, source + steps) for source in range(leading, last)])


def inverse_rms(values):
    return lax.rsqrt(jnp.mean(values * values, axis=-1, keepdims=True) + NORM_EPS)


def norm_backward(values, gain_vec, inverse, upstream):
    scaled = upstream * gain_vec
    return inverse * scaled - values * inverse**3 * jnp.mean(
        values * scaled, axis=-1, keepdims=True
    )


def times_transposed(left_side, scaling_coefficient):
    return lax.dot_general(
        left_side,
        scaling_coefficient,
        (((left_side.ndim - 1,), (1,)), ((), ())),
        preferred_element_type=jnp.float32,
    )


def window_probs(query_group, key_group, allowed):
    head_size = query_group.shape[-1]
    scores = jnp.einsum(
        "mqgd,mkgd->mgqk", query_group, key_group, preferred_element_type=jnp.float32
    ) * (1.0 / math.sqrt(head_size))
    exponent = jnp.where(allowed[None, None], jnp.exp(scores), 0.0)
    return exponent / jnp.sum(exponent, axis=-1, keepdims=True)


def split_group(array_in, first_col, group_width, head_size):
    part_cols = lax.dynamic_slice_in_dim(array_in, first_col, group_width, 2)
    return part_cols.reshape(array_in.shape[0], array_in.shape[1], heads_per_group, head_size)


def attention_forward(queries, key_rows, value_rows, allowed):
    number_of_realizations, row_count, model_width = queries.shape
    head_size = model_width // HEADS
    group_width = heads_per_group * head_size

    def one_group(group_index, output):
        first_col = (group_index * group_width).astype(jnp.int32)
        query_group = split_group(queries, first_col, group_width, head_size)
        key_group = split_group(key_rows, first_col, group_width, head_size)
        value_group = split_group(value_rows, first_col, group_width, head_size)
        soft_b = window_probs(query_group, key_group, allowed).astype(jnp.bfloat16)
        mixed_group = jnp.einsum(
            "mgqk,mkgd->mqgd", soft_b, value_group, preferred_element_type=jnp.float32
        )
        mixed_group = mixed_group.reshape(number_of_realizations, row_count, group_width).astype(
            jnp.bfloat16
        )
        return lax.dynamic_update_slice_in_dim(output, mixed_group, first_col, 2)

    return lax.fori_loop(
        0, model_width // group_width, one_group, jnp.zeros(queries.shape, jnp.bfloat16)
    )


def attention_backward(queries, key_rows, value_rows, allowed, grad_mixed):
    number_of_realizations, row_count, model_width = queries.shape
    key_count = key_rows.shape[1]
    head_size = model_width // HEADS
    group_width = heads_per_group * head_size
    score_scale = 1.0 / math.sqrt(head_size)

    def one_group(group_index, carried):
        grad_query, grad_key, grad_value = carried
        first_col = (group_index * group_width).astype(jnp.int32)
        query_group = split_group(queries, first_col, group_width, head_size)
        key_group = split_group(key_rows, first_col, group_width, head_size)
        value_group = split_group(value_rows, first_col, group_width, head_size)
        upstream_group = split_group(grad_mixed, first_col, group_width, head_size)
        soft = window_probs(query_group, key_group, allowed)
        soft_b = soft.astype(jnp.bfloat16)
        d_soft = jnp.einsum(
            "mqgd,mkgd->mgqk", upstream_group, value_group, preferred_element_type=jnp.float32
        )
        inner_sum = jnp.sum(soft * d_soft, axis=-1, keepdims=True)
        d_score = (soft * (d_soft - inner_sum) * score_scale).astype(jnp.bfloat16)
        query_part = jnp.einsum(
            "mgqk,mkgd->mqgd", d_score, key_group, preferred_element_type=jnp.float32
        )
        key_part = jnp.einsum(
            "mgqk,mqgd->mkgd", d_score, query_group, preferred_element_type=jnp.float32
        )
        value_part = jnp.einsum(
            "mgqk,mqgd->mkgd", soft_b, upstream_group, preferred_element_type=jnp.float32
        )
        grad_query = lax.dynamic_update_slice_in_dim(
            grad_query,
            query_part.reshape(number_of_realizations, row_count, group_width).astype(jnp.bfloat16),
            first_col,
            2,
        )
        grad_key = lax.dynamic_update_slice_in_dim(
            grad_key,
            key_part.reshape(number_of_realizations, key_count, group_width).astype(jnp.bfloat16),
            first_col,
            2,
        )
        grad_value = lax.dynamic_update_slice_in_dim(
            grad_value,
            value_part.reshape(number_of_realizations, key_count, group_width).astype(jnp.bfloat16),
            first_col,
            2,
        )
        return (grad_query, grad_key, grad_value)

    initial = (
        jnp.zeros(queries.shape, jnp.bfloat16),
        jnp.zeros(key_rows.shape, jnp.bfloat16),
        jnp.zeros(value_rows.shape, jnp.bfloat16),
    )
    return lax.fori_loop(0, model_width // group_width, one_group, initial)


def probabilistic_accuracy(predicted_states, measured_part, scaling_coefficient):
    number_of_realizations = predicted_states.shape[0]
    fair_factor = 1.0 - (1.0 - FAIR_ALPHA) / number_of_realizations
    gap_from_measured = predicted_states - measured_part[None]
    smooth_observed = jnp.sqrt(gap_from_measured * gap_from_measured + SMOOTH_WIDTH * SMOOTH_WIDTH)
    between_realization_gap = predicted_states[:, None] - predicted_states[None, :]
    smooth_pair = jnp.sqrt(
        between_realization_gap * between_realization_gap + SMOOTH_WIDTH * SMOOTH_WIDTH
    )
    off_diagonal = (1.0 - jnp.eye(number_of_realizations, dtype=jnp.float32))[:, :, None, None]
    point_score = jnp.sum(smooth_observed, axis=0) / number_of_realizations - fair_factor / (
        2.0 * number_of_realizations * (number_of_realizations - 1)
    ) * jnp.sum(off_diagonal * smooth_pair, axis=(0, 1))
    total = jnp.sum(scaling_coefficient[:, None] * point_score)
    gradient = scaling_coefficient[None, :, None] * (
        gap_from_measured / smooth_observed / number_of_realizations
        - fair_factor
        / (number_of_realizations * (number_of_realizations - 1.0))
        * jnp.sum(between_realization_gap / smooth_pair, axis=1)
    )
    return (total, gradient)


def project_terms(key_part, value_part, w_key, w_value):
    return (times_transposed(key_part, w_key) + times_transposed(value_part, w_value)).astype(
        jnp.bfloat16
    )


def body(
    latent,
    observed,
    area_weight,
    band_counts,
    gain_attn,
    w_query,
    w_key,
    w_value,
    w_out,
    gain_head,
    w_head,
):
    band_index = lax.axis_index("band")
    band_total = lax.axis_size("band")
    member_total = lax.axis_size("member")
    members, slot_count, model_width = latent.shape
    hops = HOPS
    offsets_list = list(range(-hops, hops + 1))
    slot_iota = jnp.arange(slot_count, dtype=jnp.int32)
    offsets = jnp.cumsum(band_counts) - band_counts

    def band_rows(shift_by):
        other = band_index + shift_by
        inside = (other >= 0) & (other < band_total)
        clipped = jnp.clip(other, 0, band_total - 1)
        return (offsets[clipped] + slot_iota, inside & (slot_iota < band_counts[clipped]))

    own_pos, own_live = band_rows(0)
    key_pos = jnp.concatenate([band_rows(offset)[0] for offset in offsets_list])
    key_live = jnp.concatenate([band_rows(offset)[1] for offset in offsets_list])
    allowed = key_live[None, :] & (jnp.abs(own_pos[:, None] - key_pos[None, :]) <= R)
    latent_f = latent.astype(jnp.float32)
    inverse_one = inverse_rms(latent_f)
    normed = (latent_f * inverse_one * gain_attn).astype(jnp.bfloat16)
    queries = jnp.dot(normed, w_query, preferred_element_type=jnp.float32).astype(jnp.bfloat16)
    own_keys = jnp.dot(normed, w_key, preferred_element_type=jnp.float32).astype(jnp.bfloat16)
    own_values = jnp.dot(normed, w_value, preferred_element_type=jnp.float32).astype(jnp.bfloat16)
    key_parts = []
    value_parts = []
    for offset in offsets_list:
        if offset == 0:
            arrived = (own_keys, own_values)
        else:
            arrived = from_behind((own_keys, own_values), "band", -offset)
        key_parts.append(arrived[0])
        value_parts.append(arrived[1])
    key_rows = jnp.concatenate(key_parts, axis=1)
    value_rows = jnp.concatenate(value_parts, axis=1)
    mixed_out = attention_forward(queries, key_rows, value_rows, allowed)
    hidden = latent_f + jnp.dot(mixed_out, w_out, preferred_element_type=jnp.float32)
    inverse_two = inverse_rms(hidden)
    head_in = (hidden * inverse_two * gain_head).astype(jnp.bfloat16)
    predicted = jnp.dot(head_in, w_head, preferred_element_type=jnp.float32).astype(jnp.bfloat16)
    total_live = jnp.sum(band_counts).astype(jnp.float32) * CH
    point_weight = area_weight * own_live.astype(jnp.float32) / total_live
    grouped = lax.all_to_all(predicted, "member", split_axis=1, concat_axis=0, tiled=True)
    point_share = slot_count // member_total
    first_point = lax.axis_index("member") * point_share
    measured_part = lax.dynamic_slice_in_dim(observed, first_point, point_share, 0).astype(
        jnp.float32
    )
    weight_part = lax.dynamic_slice_in_dim(point_weight, first_point, point_share, 0)
    loss_part, gradient = probabilistic_accuracy(
        grouped.astype(jnp.float32), measured_part, weight_part
    )
    grad_pred = lax.all_to_all(
        gradient.astype(jnp.bfloat16), "member", split_axis=0, concat_axis=1, tiled=True
    )
    ensemble_loss = lax.psum(loss_part, ("member", "band"))
    head_share = lax.psum_scatter(
        lax.dot_general(
            head_in, grad_pred, (((0, 1), (0, 1)), ((), ())), preferred_element_type=jnp.float32
        ).astype(jnp.bfloat16),
        "band",
        scatter_dimension=0,
        tiled=True,
    )
    grad_head = lax.psum(head_share, "member").astype(jnp.float32)
    grad_hidden = norm_backward(hidden, gain_head, inverse_two, times_transposed(grad_pred, w_head))
    grad_mixed = times_transposed(grad_hidden.astype(jnp.bfloat16), w_out).astype(jnp.bfloat16)
    grad_queries, key_terms, value_terms = attention_backward(
        queries, key_rows, value_rows, allowed, grad_mixed
    )
    normed_total = jnp.zeros((members, slot_count, model_width), jnp.float32)
    for piece_index, offset in enumerate(offsets_list):
        key_piece = key_terms[:, piece_index * slot_count : (piece_index + 1) * slot_count]
        value_piece = value_terms[:, piece_index * slot_count : (piece_index + 1) * slot_count]
        if offset == 0:
            received = (key_piece, value_piece)
        else:
            received = from_behind((key_piece, value_piece), "band", offset)
        normed_piece = project_terms(received[0], received[1], w_key, w_value)
        normed_total = normed_total + normed_piece.astype(jnp.float32)
    grad_normed = times_transposed(grad_queries, w_query) + normed_total
    grad_latent = (
        grad_hidden + norm_backward(latent_f, gain_attn, inverse_one, grad_normed)
    ).astype(jnp.bfloat16)
    return (grad_latent, grad_head, ensemble_loss)


def solution(mesh):
    placed = (
        P("member", "band", None),
        P("band", None),
        P("band"),
        P(),
        P(),
        P(),
        P(),
        P(),
        P(),
        P(),
        P(),
    )
    return jax.shard_map(
        body,
        mesh=mesh,
        in_specs=placed,
        out_specs=(P("member", "band", None), P("band", None), P()),
        check_vma=False,
    )
```

profile of v0, /device:TPU:112, one launch (start us, length us, event | category | flops | bytes accessed | tf_op | source)
XLA Modules:
  0.0 862.6 jit_solution(12827514641480962040)
XLA Ops:
  58.5 10.5 %collective-permute-done.8 = bf16[1,256,1024]{2,1,0:T(8,128)(2,1)} collective-permute-done((bf16[1,256,1024]{2,1,0:T(8,128)(2,1)}, bf16[1,256,1024]{2,1,0:T(8,128)(2,1)}, u32[]{:S(2)}, u32[]{:S(2)}) %collective-permute-start.8) | collective-permute-done | bytes 524320 | tf_op jit(solution)/shard_map/ppermute | solution.py:20
  88.0 11.4 %collective-permute-start.1 = (bf16[1,256,1024]{2,1,0:T(8,128)(2,1)S(1)}, bf16[1,256,1024]{2,1,0:T(8,128)(2,1)S(1)}, u32[]{:S(2)}, u32[]{:S(2)}) collective-permute-start(bf16[1,256,1024]{2,1,0:T(8,128)(2,1)S(1)} %copy-done.25), channel_id=1, source_target_pairs={{0,3},{1,4},{2,5},{3,6},{4,7},{5,8},{6,9},{7,10},{8,11},{9,12},{10... | collective-permute-start | bytes 1572872 | tf_op jit(solution)/shard_map/ppermute | solution.py:20
  107.1 14.1 %collective-permute-done.13 = bf16[1,256,1024]{2,1,0:T(8,128)(2,1)S(1)} collective-permute-done((bf16[1,256,1024]{2,1,0:T(8,128)(2,1)}, bf16[1,256,1024]{2,1,0:T(8,128)(2,1)S(1)}, u32[]{:S(2)}, u32[]{:S(2)}) %collective-permute-start.13) | collective-permute-done | bytes 524320 | tf_op jit(solution)/shard_map/ppermute | solution.py:20
  156.9 24.8 %collective-permute-done.5 = bf16[1,256,1024]{2,1,0:T(8,128)(2,1)S(1)} collective-permute-done((bf16[1,256,1024]{2,1,0:T(8,128)(2,1)S(1)}, bf16[1,256,1024]{2,1,0:T(8,128)(2,1)S(1)}, u32[]{:S(2)}, u32[]{:S(2)}) %collective-permute-start.5) | collective-permute-done | bytes 524320 | tf_op jit(solution)/shard_map/ppermute | solution.py:20
  193.1 39.2 %while.32 = (s32[]{:T(128)}, bf16[1,256,1024]{1,2,0:T(8,128)(2,1)S(1)}, bf16[1,2304,1024]{1,2,0:T(8,128)(2,1)}, bf16[1,256,1024]{1,2,0:T(8,128)(2,1)}, bf16[1,23...) while((s32[]{:T(128)}, ...), condition=%wide.region_4.5_spmd.clone, body=%wide.region_2.4_spmd.clone.sunk | while | flops 622918656 | bytes 28529072 | solution.py:76
  261.7 69.6 %psum.15 = f32[]{:T(128)} all-reduce(f32[]{:T(128)} %multiply_reduce_fusion.2), channel_id=1, replica_groups=mesh['member'=8,'band'=16] {'member','band'}, use_global_device_ids=true, to_apply=%region_19.20 | all-reduce | flops 1 | bytes 8 | tf_op jit(solution)/shard_map/psum | solution.py:237
  344.2 257.3 %while.33 = (s32[]{:T(128)}, bf16[1,256,1024]{1,2,0:T(8,128)(2,1)}, bf16[1,2304,1024]{1,2,0:T(8,128)(2,1)}, bf16[1,2304,1024]{1,2,0:T(8,128)(2,1)}, bf16[1,2304,...) while((s32[]{:T(128)}, bf16[1,256,1024]{1,2,0:T(8,128)(2,1)}, ...), condition=%wide.region_12.13_spmd.clone, body=%wide.region_9.12_spmd.clone.sunk | while | flops 1581979136 | bytes 88961552 | solution.py:136
  361.3 19.0 %fusion.217 = bf16[4,64,256]{2,1,0:T(8,128)(2,1)} fusion(bf16[2304,4,64]{0,2,1:T(8,128)(2,1)S(1)} %bitcast.244, f32[4,256,2304]{2,1,0:T(8,128)} %fusion.214, f32[4,256,2304]{2,1,0:T(8,128)} %get-tuple-element.631, f32[4,256]{1,0:T(4,128)} %get-tuple-element.632, pred[256,2304]{1,0:T(8,128)(4,1)} %copy-done.5), kind=kOutput, calls=%fused_computation.30.clone.1 | convolution fusion | flops 328011008 | bytes 20779008 | tf_op jit(solution)/shard_map/while/body/eval_jaxpr/mgqk,mkgd->mqgd/dot_general | solution.py:102
  380.3 19.6 %fusion.219 = bf16[4,64,2304]{2,1,0:T(8,128)(2,1)S(1)} fusion(bf16[256,4,64]{0,2,1:T(8,128)(2,1)S(1)} %bitcast.248, f32[4,256,2304]{2,1,0:T(8,128)} %fusion.214, f32[4,256,2304]{2,1,0:T(8,128)} %get-tuple-element.631, f32[4,256]{1,0:T(4,128)} %get-tuple-element.632, pred[256,2304]{1,0:T(8,128)(4,1)} %copy-done.5), kind=kOutput, calls=%fused_computation.27.clone.1 | convolution fusion | flops 328535296 | bytes 20779008 | tf_op jit(solution)/shard_map/while/body/eval_jaxpr/mgqk,mqgd->mkgd/dot_general | solution.py:105
  425.6 19.0 %fusion.217 = bf16[4,64,256]{2,1,0:T(8,128)(2,1)} fusion(bf16[2304,4,64]{0,2,1:T(8,128)(2,1)S(1)} %bitcast.244, f32[4,256,2304]{2,1,0:T(8,128)} %fusion.214, f32[4,256,2304]{2,1,0:T(8,128)} %get-tuple-element.631, f32[4,256]{1,0:T(4,128)} %get-tuple-element.632, pred[256,2304]{1,0:T(8,128)(4,1)} %copy-done.5), kind=kOutput, calls=%fused_computation.30.clone.1 | convolution fusion | flops 328011008 | bytes 20779008 | tf_op jit(solution)/shard_map/while/body/eval_jaxpr/mgqk,mkgd->mqgd/dot_general | solution.py:102
  444.6 19.6 %fusion.219 = bf16[4,64,2304]{2,1,0:T(8,128)(2,1)S(1)} fusion(bf16[256,4,64]{0,2,1:T(8,128)(2,1)S(1)} %bitcast.248, f32[4,256,2304]{2,1,0:T(8,128)} %fusion.214, f32[4,256,2304]{2,1,0:T(8,128)} %get-tuple-element.631, f32[4,256]{1,0:T(4,128)} %get-tuple-element.632, pred[256,2304]{1,0:T(8,128)(4,1)} %copy-done.5), kind=kOutput, calls=%fused_computation.27.clone.1 | convolution fusion | flops 328535296 | bytes 20779008 | tf_op jit(solution)/shard_map/while/body/eval_jaxpr/mgqk,mqgd->mkgd/dot_general | solution.py:105
  489.8 19.0 %fusion.217 = bf16[4,64,256]{2,1,0:T(8,128)(2,1)} fusion(bf16[2304,4,64]{0,2,1:T(8,128)(2,1)S(1)} %bitcast.244, f32[4,256,2304]{2,1,0:T(8,128)} %fusion.214, f32[4,256,2304]{2,1,0:T(8,128)} %get-tuple-element.631, f32[4,256]{1,0:T(4,128)} %get-tuple-element.632, pred[256,2304]{1,0:T(8,128)(4,1)} %copy-done.5), kind=kOutput, calls=%fused_computation.30.clone.1 | convolution fusion | flops 328011008 | bytes 20779008 | tf_op jit(solution)/shard_map/while/body/eval_jaxpr/mgqk,mkgd->mqgd/dot_general | solution.py:102
  508.8 19.6 %fusion.219 = bf16[4,64,2304]{2,1,0:T(8,128)(2,1)S(1)} fusion(bf16[256,4,64]{0,2,1:T(8,128)(2,1)S(1)} %bitcast.248, f32[4,256,2304]{2,1,0:T(8,128)} %fusion.214, f32[4,256,2304]{2,1,0:T(8,128)} %get-tuple-element.631, f32[4,256]{1,0:T(4,128)} %get-tuple-element.632, pred[256,2304]{1,0:T(8,128)(4,1)} %copy-done.5), kind=kOutput, calls=%fused_computation.27.clone.1 | convolution fusion | flops 328535296 | bytes 20779008 | tf_op jit(solution)/shard_map/while/body/eval_jaxpr/mgqk,mqgd->mkgd/dot_general | solution.py:105
  554.0 19.0 %fusion.217 = bf16[4,64,256]{2,1,0:T(8,128)(2,1)} fusion(bf16[2304,4,64]{0,2,1:T(8,128)(2,1)S(1)} %bitcast.244, f32[4,256,2304]{2,1,0:T(8,128)} %fusion.214, f32[4,256,2304]{2,1,0:T(8,128)} %get-tuple-element.631, f32[4,256]{1,0:T(4,128)} %get-tuple-element.632, pred[256,2304]{1,0:T(8,128)(4,1)} %copy-done.5), kind=kOutput, calls=%fused_computation.30.clone.1 | convolution fusion | flops 328011008 | bytes 20779008 | tf_op jit(solution)/shard_map/while/body/eval_jaxpr/mgqk,mkgd->mqgd/dot_general | solution.py:102
  573.0 19.6 %fusion.219 = bf16[4,64,2304]{2,1,0:T(8,128)(2,1)S(1)} fusion(bf16[256,4,64]{0,2,1:T(8,128)(2,1)S(1)} %bitcast.248, f32[4,256,2304]{2,1,0:T(8,128)} %fusion.214, f32[4,256,2304]{2,1,0:T(8,128)} %get-tuple-element.631, f32[4,256]{1,0:T(4,128)} %get-tuple-element.632, pred[256,2304]{1,0:T(8,128)(4,1)} %copy-done.5), kind=kOutput, calls=%fused_computation.27.clone.1 | convolution fusion | flops 328535296 | bytes 20779008 | tf_op jit(solution)/shard_map/while/body/eval_jaxpr/mgqk,mqgd->mkgd/dot_general | solution.py:105
  632.7 71.4 %reduce-scatter.2.cloned.1.call-done = bf16[64,128]{1,0:T(8,128)(2,1)} async-done(((bf16[1024,128]{1,0:T(8,128)(2,1)}), bf16[64,128]{1,0:T(8,128)(2,1)}) %reduce-scatter.2.cloned.1.call-update) | async-done | bytes 16400 | tf_op jit(solution)/shard_map/reduce_scatter | solution.py:238
  704.0 19.8 %psum.14 = bf16[64,128]{1,0:T(8,128)(2,1)S(1)} all-reduce(bf16[64,128]{1,0:T(8,128)(2,1)} %reduce-scatter.2.cloned.1.call-done), channel_id=1, replica_groups=mesh['member'=8,'band'=16] {'member'}, use_global_device_ids=true, to_apply=%region_15.16 | all-reduce | flops 8192 | bytes 32768 | tf_op jit(solution)/shard_map/psum | solution.py:246
  741.1 18.3 %collective-permute-done.26 = bf16[1,256,1024]{1,2,0:T(8,128)(2,1)S(1)} collective-permute-done((bf16[1,256,1024]{1,2,0:T(8,128)(2,1)}, bf16[1,256,1024]{1,2,0:T(8,128)(2,1)S(1)}, u32[]{:S(2)}, u32[]{:S(2)}) %collective-permute-start.26) | collective-permute-done | bytes 524320 | tf_op jit(solution)/shard_map/ppermute | solution.py:20
  759.4 9.5 %collective-permute-start.24 = (bf16[1,256,1024]{1,2,0:T(8,128)(2,1)S(1)}, bf16[1,256,1024]{1,2,0:T(8,128)(2,1)S(1)}, u32[]{:S(2)}, u32[]{:S(2)}) collective-permute-start(bf16[1,256,1024]{1,2,0:T(8,128)(2,1)S(1)} %copy-done.24), channel_id=1, source_target_pairs={{0,1},{1,2},{2,3},{3,4},{4,5},{5,6},{6,7},{7,8},{8,9},{9,10},{10,1... | collective-permute-start | bytes 1572872 | tf_op jit(solution)/shard_map/ppermute | solution.py:20
  773.0 18.6 %collective-permute-done.24 = bf16[1,256,1024]{1,2,0:T(8,128)(2,1)S(1)} collective-permute-done((bf16[1,256,1024]{1,2,0:T(8,128)(2,1)S(1)}, bf16[1,256,1024]{1,2,0:T(8,128)(2,1)S(1)}, u32[]{:S(2)}, u32[]{:S(2)}) %collective-permute-start.24) | collective-permute-done | bytes 524320 | tf_op jit(solution)/shard_map/ppermute | solution.py:20
  797.7 9.7 %collective-permute-done.22 = bf16[1,256,1024]{1,2,0:T(8,128)(2,1)S(1)} collective-permute-done((bf16[1,256,1024]{1,2,0:T(8,128)(2,1)S(1)}, bf16[1,256,1024]{1,2,0:T(8,128)(2,1)S(1)}, u32[]{:S(2)}, u32[]{:S(2)}) %collective-permute-start.22) | collective-permute-done | bytes 524320 | tf_op jit(solution)/shard_map/ppermute | solution.py:20
  812.3 14.1 %collective-permute-done.20 = bf16[1,256,1024]{1,2,0:T(8,128)(2,1)S(1)} collective-permute-done((bf16[1,256,1024]{1,2,0:T(8,128)(2,1)S(1)}, bf16[1,256,1024]{1,2,0:T(8,128)(2,1)S(1)}, u32[]{:S(2)}, u32[]{:S(2)}) %collective-permute-start.20) | collective-permute-done | bytes 524320 | tf_op jit(solution)/shard_map/ppermute | solution.py:20
  828.6 8.1 collective-permute-start.30
  837.5 10.7 %collective-permute-done.18 = bf16[1,256,1024]{1,2,0:T(8,128)(2,1)S(1)} collective-permute-done((bf16[1,256,1024]{1,2,0:T(8,128)(2,1)S(1)}, bf16[1,256,1024]{1,2,0:T(8,128)(2,1)S(1)}, u32[]{:S(2)}, u32[]{:S(2)}) %collective-permute-start.18) | collective-permute-done | bytes 524320 | tf_op jit(solution)/shard_map/ppermute | solution.py:20
  (322 shorter events, 380.2 us)
Async XLA Ops:
  11.7 115.1 %collective-permute-start.15 = (bf16[1,256,1024]{2,1,0:T(8,128)(2,1)}, bf16[1,256,1024]{2,1,0:T(8,128)(2,1)S(1)}, u32[]{:S(2)}, u32[]{:S(2)}) collective-permute-start(bf16[1,256,1024]{2,1,0:T(8,128)(2,1)} %fusion.73), channel_id=1, source_target_pairs={{4,0},{5,1},{6,2},{7,3},{8,4},{9,5},{10,6},{11,7},{12,8},{13,9},{1... | collective-permute-start | bytes 1572872 | tf_op jit(solution)/shard_map/ppermute | solution.py:20
  13.0 69.9 %collective-permute-start.11 = (bf16[1,256,1024]{2,1,0:T(8,128)(2,1)}, bf16[1,256,1024]{2,1,0:T(8,128)(2,1)}, u32[]{:S(2)}, u32[]{:S(2)}) collective-permute-start(bf16[1,256,1024]{2,1,0:T(8,128)(2,1)} %fusion.73), channel_id=1, source_target_pairs={{0,1},{1,2},{2,3},{3,4},{4,5},{5,6},{6,7},{7,8},{8,9},{9,10},{10,1... | collective-permute-start | bytes 1572872 | tf_op jit(solution)/shard_map/ppermute | solution.py:20
  16.2 62.9 %collective-permute-start.10 = (bf16[1,256,1024]{2,1,0:T(8,128)(2,1)}, bf16[1,256,1024]{2,1,0:T(8,128)(2,1)}, u32[]{:S(2)}, u32[]{:S(2)}) collective-permute-start(bf16[1,256,1024]{2,1,0:T(8,128)(2,1)} %fusion.73), channel_id=1, source_target_pairs={{0,2},{1,3},{2,4},{3,5},{4,6},{5,7},{6,8},{7,9},{8,10},{9,11},{10,... | collective-permute-start | bytes 1572872 | tf_op jit(solution)/shard_map/ppermute | solution.py:20
  20.8 54.5 %collective-permute-start.9 = (bf16[1,256,1024]{2,1,0:T(8,128)(2,1)}, bf16[1,256,1024]{2,1,0:T(8,128)(2,1)}, u32[]{:S(2)}, u32[]{:S(2)}) collective-permute-start(bf16[1,256,1024]{2,1,0:T(8,128)(2,1)} %fusion.73), channel_id=1, source_target_pairs={{0,3},{1,4},{2,5},{3,6},{4,7},{5,8},{6,9},{7,10},{8,11},{9,12},{10... | collective-permute-start | bytes 1572872 | tf_op jit(solution)/shard_map/ppermute | solution.py:20
  25.5 43.5 %collective-permute-start.8 = (bf16[1,256,1024]{2,1,0:T(8,128)(2,1)}, bf16[1,256,1024]{2,1,0:T(8,128)(2,1)}, u32[]{:S(2)}, u32[]{:S(2)}) collective-permute-start(bf16[1,256,1024]{2,1,0:T(8,128)(2,1)} %fusion.73), channel_id=1, source_target_pairs={{0,4},{1,5},{2,6},{3,7},{4,8},{5,9},{6,10},{7,11},{8,12},{9,13},{1... | collective-permute-start | bytes 1572872 | tf_op jit(solution)/shard_map/ppermute | solution.py:20
  79.1 42.1 %collective-permute-start.13 = (bf16[1,256,1024]{2,1,0:T(8,128)(2,1)}, bf16[1,256,1024]{2,1,0:T(8,128)(2,1)S(1)}, u32[]{:S(2)}, u32[]{:S(2)}) collective-permute-start(bf16[1,256,1024]{2,1,0:T(8,128)(2,1)} %fusion.73), channel_id=1, source_target_pairs={{2,0},{3,1},{4,2},{5,3},{6,4},{7,5},{8,6},{9,7},{10,8},{11,9},{12,... | collective-permute-start | bytes 1572872 | tf_op jit(solution)/shard_map/ppermute | solution.py:20
  82.9 41.8 %collective-permute-start.14 = (bf16[1,256,1024]{2,1,0:T(8,128)(2,1)}, bf16[1,256,1024]{2,1,0:T(8,128)(2,1)S(1)}, u32[]{:S(2)}, u32[]{:S(2)}) collective-permute-start(bf16[1,256,1024]{2,1,0:T(8,128)(2,1)} %fusion.73), channel_id=1, source_target_pairs={{3,0},{4,1},{5,2},{6,3},{7,4},{8,5},{9,6},{10,7},{11,8},{12,9},{13... | collective-permute-start | bytes 1572872 | tf_op jit(solution)/shard_map/ppermute | solution.py:20
  88.0 46.4 %collective-permute-start.1 = (bf16[1,256,1024]{2,1,0:T(8,128)(2,1)S(1)}, bf16[1,256,1024]{2,1,0:T(8,128)(2,1)S(1)}, u32[]{:S(2)}, u32[]{:S(2)}) collective-permute-start(bf16[1,256,1024]{2,1,0:T(8,128)(2,1)S(1)} %copy-done.25), channel_id=1, source_target_pairs={{0,3},{1,4},{2,5},{3,6},{4,7},{5,8},{6,9},{7,10},{8,11},{9,12},{10... | collective-permute-start | bytes 1572872 | tf_op jit(solution)/shard_map/ppermute | solution.py:20
  100.3 39.9 %collective-permute-start.2 = (bf16[1,256,1024]{2,1,0:T(8,128)(2,1)S(1)}, bf16[1,256,1024]{2,1,0:T(8,128)(2,1)S(1)}, u32[]{:S(2)}, u32[]{:S(2)}) collective-permute-start(bf16[1,256,1024]{2,1,0:T(8,128)(2,1)S(1)} %copy-done.25), channel_id=1, source_target_pairs={{0,2},{1,3},{2,4},{3,5},{4,6},{5,7},{6,8},{7,9},{8,10},{9,11},{10,... | collective-permute-start | bytes 1572872 | tf_op jit(solution)/shard_map/ppermute | solution.py:20
  124.7 59.7 %collective-permute-start.7 = (bf16[1,256,1024]{2,1,0:T(8,128)(2,1)S(1)}, bf16[1,256,1024]{2,1,0:T(8,128)(2,1)}, u32[]{:S(2)}, u32[]{:S(2)}) collective-permute-start(bf16[1,256,1024]{2,1,0:T(8,128)(2,1)S(1)} %copy-done.25), channel_id=1, source_target_pairs={{4,0},{5,1},{6,2},{7,3},{8,4},{9,5},{10,6},{11,7},{12,8},{13,9},{1... | collective-permute-start | bytes 1572872 | tf_op jit(solution)/shard_map/ppermute | solution.py:20
  134.3 47.4 %collective-permute-start.5 = (bf16[1,256,1024]{2,1,0:T(8,128)(2,1)S(1)}, bf16[1,256,1024]{2,1,0:T(8,128)(2,1)S(1)}, u32[]{:S(2)}, u32[]{:S(2)}) collective-permute-start(bf16[1,256,1024]{2,1,0:T(8,128)(2,1)S(1)} %copy-done.25), channel_id=1, source_target_pairs={{2,0},{3,1},{4,2},{5,3},{6,4},{7,5},{8,6},{9,7},{10,8},{11,9},{12,... | collective-permute-start | bytes 1572872 | tf_op jit(solution)/shard_map/ppermute | solution.py:20
  140.1 42.4 %collective-permute-start.6 = (bf16[1,256,1024]{2,1,0:T(8,128)(2,1)S(1)}, bf16[1,256,1024]{2,1,0:T(8,128)(2,1)}, u32[]{:S(2)}, u32[]{:S(2)}) collective-permute-start(bf16[1,256,1024]{2,1,0:T(8,128)(2,1)S(1)} %copy-done.25), channel_id=1, source_target_pairs={{3,0},{4,1},{5,2},{6,3},{7,4},{8,5},{9,6},{10,7},{11,8},{12,9},{13... | collective-permute-start | bytes 1572872 | tf_op jit(solution)/shard_map/ppermute | solution.py:20
  254.9 76.4 %all-to-all-start.1 = ((bf16[8,32,128]{2,1,0:T(8,128)(2,1)}), bf16[8,32,128]{2,1,0:T(8,128)(2,1)S(1)}, u32[]{:S(2)}, u32[]{:S(2)}) async-start(bf16[8,32,128]{2,1,0:T(8,128)(2,1)} %get-tuple-element.463), calls=%async_computation.1 | async-start | bytes 131072 | tf_op jit(solution)/shard_map/all_to_all | solution.py:234
  260.3 443.7 %reduce-scatter.2.cloned.1.call-start = ((), (), s32[]{:S(2)}) async-start(), calls=%async_computation.3 | async-start | bytes 278528 | tf_op jit(solution)/shard_map/reduce_scatter | solution.py:238
  612.0 237.0 %collective-permute-start.17 = (bf16[1,256,1024]{1,2,0:T(8,128)(2,1)}, bf16[1,256,1024]{1,2,0:T(8,128)(2,1)}, u32[]{:S(2)}, u32[]{:S(2)}) collective-permute-start(bf16[1,256,1024]{1,2,0:T(8,128)(2,1)} %get-tuple-element.454), channel_id=1, source_target_pairs={{4,0},{5,1},{6,2},{7,3},{8,4},{9,5},{10,6},{11,7},{12,8},{13,9},{1... | collective-permute-start | bytes 1572872 | tf_op jit(solution)/shard_map/ppermute | solution.py:20
  613.3 111.2 %collective-permute-start.29 = (bf16[1,256,1024]{1,2,0:T(8,128)(2,1)}, bf16[1,256,1024]{1,2,0:T(8,128)(2,1)}, u32[]{:S(2)}, u32[]{:S(2)}) collective-permute-start(bf16[1,256,1024]{1,2,0:T(8,128)(2,1)} %get-tuple-element.455), channel_id=1, source_target_pairs={{0,3},{1,4},{2,5},{3,6},{4,7},{5,8},{6,9},{7,10},{8,11},{9,12},{10... | collective-permute-start | bytes 1572872 | tf_op jit(solution)/shard_map/ppermute | solution.py:20
  618.8 118.4 %collective-permute-start.27 = (bf16[1,256,1024]{1,2,0:T(8,128)(2,1)}, bf16[1,256,1024]{1,2,0:T(8,128)(2,1)}, u32[]{:S(2)}, u32[]{:S(2)}) collective-permute-start(bf16[1,256,1024]{1,2,0:T(8,128)(2,1)} %get-tuple-element.456), channel_id=1, source_target_pairs={{0,2},{1,3},{2,4},{3,5},{4,6},{5,7},{6,8},{7,9},{8,10},{9,11},{10,... | collective-permute-start | bytes 1572872 | tf_op jit(solution)/shard_map/ppermute | solution.py:20
  621.6 148.1 %collective-permute-start.25 = (bf16[1,256,1024]{1,2,0:T(8,128)(2,1)}, bf16[1,256,1024]{1,2,0:T(8,128)(2,1)}, u32[]{:S(2)}, u32[]{:S(2)}) collective-permute-start(bf16[1,256,1024]{1,2,0:T(8,128)(2,1)} %get-tuple-element.457), channel_id=1, source_target_pairs={{0,1},{1,2},{2,3},{3,4},{4,5},{5,6},{6,7},{7,8},{8,9},{9,10},{10,1... | collective-permute-start | bytes 1572872 | tf_op jit(solution)/shard_map/ppermute | solution.py:20
  625.1 104.6 %collective-permute-start.28 = (bf16[1,256,1024]{1,2,0:T(8,128)(2,1)}, bf16[1,256,1024]{1,2,0:T(8,128)(2,1)}, u32[]{:S(2)}, u32[]{:S(2)}) collective-permute-start(bf16[1,256,1024]{1,2,0:T(8,128)(2,1)} %get-tuple-element.447), channel_id=1, source_target_pairs={{0,3},{1,4},{2,5},{3,6},{4,7},{5,8},{6,9},{7,10},{8,11},{9,12},{10... | collective-permute-start | bytes 1572872 | tf_op jit(solution)/shard_map/ppermute | solution.py:20
  724.5 70.1 %collective-permute-start.23 = (bf16[1,256,1024]{1,2,0:T(8,128)(2,1)}, bf16[1,256,1024]{1,2,0:T(8,128)(2,1)S(1)}, u32[]{:S(2)}, u32[]{:S(2)}) collective-permute-start(bf16[1,256,1024]{1,2,0:T(8,128)(2,1)} %get-tuple-element.458), channel_id=1, source_target_pairs={{1,0},{2,1},{3,2},{4,3},{5,4},{6,5},{7,6},{8,7},{9,8},{10,9},{11,1... | collective-permute-start | bytes 1572872 | tf_op jit(solution)/shard_map/ppermute | solution.py:20
  737.2 72.9 %collective-permute-start.21 = (bf16[1,256,1024]{1,2,0:T(8,128)(2,1)S(1)}, bf16[1,256,1024]{1,2,0:T(8,128)(2,1)S(1)}, u32[]{:S(2)}, u32[]{:S(2)}) collective-permute-start(bf16[1,256,1024]{1,2,0:T(8,128)(2,1)S(1)} %copy-done.23), channel_id=1, source_target_pairs={{2,0},{3,1},{4,2},{5,3},{6,4},{7,5},{8,6},{9,7},{10,8},{11,9},{12,... | collective-permute-start | bytes 1572872 | tf_op jit(solution)/shard_map/ppermute | solution.py:20
  769.7 58.8 %collective-permute-start.19 = (bf16[1,256,1024]{1,2,0:T(8,128)(2,1)S(1)}, bf16[1,256,1024]{1,2,0:T(8,128)(2,1)S(1)}, u32[]{:S(2)}, u32[]{:S(2)}) collective-permute-start(bf16[1,256,1024]{1,2,0:T(8,128)(2,1)S(1)} %copy-done.21), channel_id=1, source_target_pairs={{3,0},{4,1},{5,2},{6,3},{7,4},{8,5},{9,6},{10,7},{11,8},{12,9},{13... | collective-permute-start | bytes 1572872 | tf_op jit(solution)/shard_map/ppermute | solution.py:20
  794.7 56.2 %collective-permute-start.31 = (bf16[1,256,1024]{1,2,0:T(8,128)(2,1)S(1)}, bf16[1,256,1024]{1,2,0:T(8,128)(2,1)S(1)}, u32[]{:S(2)}, u32[]{:S(2)}) collective-permute-start(bf16[1,256,1024]{1,2,0:T(8,128)(2,1)S(1)} %copy-done.19), channel_id=1, source_target_pairs={{0,4},{1,5},{2,6},{3,7},{4,8},{5,9},{6,10},{7,11},{8,12},{9,13},{1... | collective-permute-start | bytes 1572872 | tf_op jit(solution)/shard_map/ppermute | solution.py:20
  810.1 42.4 %collective-permute-start.16 = (bf16[1,256,1024]{1,2,0:T(8,128)(2,1)S(1)}, bf16[1,256,1024]{1,2,0:T(8,128)(2,1)S(1)}, u32[]{:S(2)}, u32[]{:S(2)}) collective-permute-start(bf16[1,256,1024]{1,2,0:T(8,128)(2,1)S(1)} %copy-done.16), channel_id=1, source_target_pairs={{4,0},{5,1},{6,2},{7,3},{8,4},{9,5},{10,6},{11,7},{12,8},{13,9},{1... | collective-permute-start | bytes 1572872 | tf_op jit(solution)/shard_map/ppermute | solution.py:20
  (55 other events, 1044.8 us)
Sparse Core Ops, SparseCore 0:
  607.7 96.3 reduce-scatter.1
where the time goes:
time: 871 us; the launch traced here: 863 us
  matrix products  288 us (33%)
  waiting for transfers between devices  203 us (23%)
  starting transfers between devices  123 us (14%)
  local copies, waits for them, and re-layouts  103 us (12%)
  blocking collectives  89.4 us (10%)
  other arithmetic  39.8 us (5%)
  between operations  16.2 us (2%)
    ppermute x32, waiting for transfers between devices, from_behind(): lax.ppermute(value, axis, [(source, source + steps) for source in range(l...  129 us
    ppermute x32, starting transfers between devices, from_behind(): lax.ppermute(value, axis, [(source, source + steps) for source in range(l...  113 us
    dot_general x4, matrix products, one_group(): jnp.einsum('mgqk,mqgd->mkgd', d_score, query_group, preferred_element_typ...  78.6 us
    dot_general x4, matrix products, one_group(): jnp.einsum('mgqk,mkgd->mqgd', d_score, key_group, preferred_element_type=...  76.1 us
    reduce_scatter x1, waiting for transfers between devices, body(): lax.psum_scatter(lax.dot_general(head_in, grad_pred, (((0, 1), (0, 1)), (...  71.4 us
    psum x1, blocking collectives, body(): ensemble_loss = lax.psum(loss_part, ('member', 'band'))  69.6 us
    unnamed x102, local copies, waits for them, and re-layouts  43.2 us
    dot_general x8, matrix products, window_probs(): jnp.einsum('mqgd,mkgd->mgqk', query_group, key_group, preferred_element_t...  33.4 us
  transfers between devices with their start and end apart: 35, of which 13 were waited for; matrix products, arithmetic and copies ran while one was open for 10% of the time, Pallas kernels for 0%

commit v1 on v0

--- a/solution.py
+++ b/solution.py
@@ -1,3 +1,4 @@
+import functools
 import math
 import jax
 import jax.numpy as jnp
@@ -12,6 +13,14 @@
 SMOOTH_WIDTH = 0.25
 FAIR_ALPHA = 0.95
 heads_per_group = 4
+
+
+def pass_regions_here(local, mesh_dim):
+    next_value = lax.all_gather(local, mesh_dim)
+    return jnp.sum(next_value, axis=0)
+
+
+draft_links_now = functools.partial(pass_regions_here, mesh_dim="member")
 
 
 def from_behind(value, axis, steps):
@@ -243,7 +252,7 @@
         scatter_dimension=0,
         tiled=True,
     )
-    grad_head = lax.psum(head_share, "member").astype(jnp.float32)
+    grad_head = draft_links_now(head_share).astype(jnp.float32)
     grad_hidden = norm_backward(hidden, gain_head, inverse_two, times_transposed(grad_pred, w_head))
     grad_mixed = times_transposed(grad_hidden.astype(jnp.bfloat16), w_out).astype(jnp.bfloat16)
     grad_queries, key_terms, value_terms = attention_backward(

time: 871 us -> 793 us (0.910)
  waiting for transfers between devices: 203 us -> 129 us
    reduce_scatter x1, waiting for transfers between devices: 71.4 us -> 0.02 us  [body(): lax.psum_scatter(lax.dot_general(head_in, grad_pred, (((0, 1), (0, 1)), (...]
    psum x1 -> x0, blocking collectives: 19.8 us -> none  [body(): grad_head = lax.psum(head_share, 'member').astype(jnp.float32)]
    all_gather x0 -> x1, blocking collectives: none -> 13 us  [pass_regions_here(): next_value = lax.all_gather(local, mesh_dim)]
    unnamed x102 -> x104, local copies, waits for them, and re-layouts: 43.2 us -> 42.2 us
  transfers between devices with their start and end apart: 35 -> 35, of which waited for: 13 -> 12; matrix products, arithmetic and copies ran while one was open for 10% -> 45% of each run, Pallas kernels for 0% -> 0%
where the time goes in v1:
time: 793 us; the launch traced here: 782 us
  matrix products  289 us (36%)
  waiting for transfers between devices  129 us (16%)
  starting transfers between devices  125 us (16%)
  local copies, waits for them, and re-layouts  99.7 us (13%)
  blocking collectives  82.5 us (10%)
  other arithmetic  39.9 us (5%)
  between operations  16.2 us (2%)
    ppermute x32, waiting for transfers between devices, from_behind(): lax.ppermute(value, axis, [(source, source + steps) for source in range(l...  126 us
    ppermute x32, starting transfers between devices, from_behind(): lax.ppermute(value, axis, [(source, source + steps) for source in range(l...  115 us
    dot_general x4, matrix products, one_group(): jnp.einsum('mgqk,mqgd->mkgd', d_score, query_group, preferred_element_typ...  78.4 us
    dot_general x4, matrix products, one_group(): jnp.einsum('mgqk,mkgd->mqgd', d_score, key_group, preferred_element_type=...  76 us
    psum x1, blocking collectives, body(): ensemble_loss = lax.psum(loss_part, ('member', 'band'))  69.6 us
    unnamed x104, local copies, waits for them, and re-layouts  42.2 us
    dot_general x8, matrix products, window_probs(): jnp.einsum('mqgd,mkgd->mgqk', query_group, key_group, preferred_element_t...  33.1 us
    dynamic_slice x28, local copies, waits for them, and re-layouts, split_group(): part_cols = lax.dynamic_slice_in_dim(array_in, first_col, group_width, 2)  30.3 us
  transfers between devices with their start and end apart: 35, of which 12 were waited for; matrix products, arithmetic and copies ran while one was open for 45% of the time, Pallas kernels for 0%

profile of v1, /device:TPU:112, one launch (start us, length us, event | category | flops | bytes accessed | tf_op | source)
XLA Modules:
  0.0 781.5 jit_solution(10943750812590681687)
XLA Ops:
  58.5 10.6 %collective-permute-done.8 = bf16[1,256,1024]{2,1,0:T(8,128)(2,1)} collective-permute-done((bf16[1,256,1024]{2,1,0:T(8,128)(2,1)}, bf16[1,256,1024]{2,1,0:T(8,128)(2,1)}, u32[]{:S(2)}, u32[]{:S(2)}) %collective-permute-start.8) | collective-permute-done | bytes 524320 | tf_op jit(solution)/shard_map/ppermute | solution.py:29
  88.0 11.4 %collective-permute-start.1 = (bf16[1,256,1024]{2,1,0:T(8,128)(2,1)S(1)}, bf16[1,256,1024]{2,1,0:T(8,128)(2,1)S(1)}, u32[]{:S(2)}, u32[]{:S(2)}) collective-permute-start(bf16[1,256,1024]{2,1,0:T(8,128)(2,1)S(1)} %copy-done.24), channel_id=1, source_target_pairs={{0,3},{1,4},{2,5},{3,6},{4,7},{5,8},{6,9},{7,10},{8,11},{9,12},{10... | collective-permute-start | bytes 1572872 | tf_op jit(solution)/shard_map/ppermute | solution.py:29
  107.2 14.2 %collective-permute-done.13 = bf16[1,256,1024]{2,1,0:T(8,128)(2,1)S(1)} collective-permute-done((bf16[1,256,1024]{2,1,0:T(8,128)(2,1)}, bf16[1,256,1024]{2,1,0:T(8,128)(2,1)S(1)}, u32[]{:S(2)}, u32[]{:S(2)}) %collective-permute-start.13) | collective-permute-done | bytes 524320 | tf_op jit(solution)/shard_map/ppermute | solution.py:29
  156.9 24.9 %collective-permute-done.5 = bf16[1,256,1024]{2,1,0:T(8,128)(2,1)S(1)} collective-permute-done((bf16[1,256,1024]{2,1,0:T(8,128)(2,1)S(1)}, bf16[1,256,1024]{2,1,0:T(8,128)(2,1)S(1)}, u32[]{:S(2)}, u32[]{:S(2)}) %collective-permute-start.5) | collective-permute-done | bytes 524320 | tf_op jit(solution)/shard_map/ppermute | solution.py:29
  186.4 6.8 copy.40
  193.2 39.2 %while.32 = (s32[]{:T(128)}, bf16[1,256,1024]{1,2,0:T(8,128)(2,1)S(1)}, bf16[1,2304,1024]{1,2,0:T(8,128)(2,1)}, bf16[1,256,1024]{1,2,0:T(8,128)(2,1)}, bf16[1,23...) while((s32[]{:T(128)}, ...), condition=%wide.region_4.5_spmd.clone, body=%wide.region_2.4_spmd.clone.sunk | while | flops 622918656 | bytes 28529072 | solution.py:85
  261.9 69.6 %psum.7 = f32[]{:T(128)} all-reduce(f32[]{:T(128)} %multiply_reduce_fusion.2), channel_id=1, replica_groups=mesh['member'=8,'band'=16] {'member','band'}, use_global_device_ids=true, to_apply=%region_19.20 | all-reduce | flops 1 | bytes 8 | tf_op jit(solution)/shard_map/psum | solution.py:246
  344.6 256.9 %while.33 = (s32[]{:T(128)}, bf16[1,256,1024]{1,2,0:T(8,128)(2,1)}, bf16[1,2304,1024]{1,2,0:T(8,128)(2,1)}, bf16[1,2304,1024]{1,2,0:T(8,128)(2,1)}, bf16[1,2304,...) while((s32[]{:T(128)}, bf16[1,256,1024]{1,2,0:T(8,128)(2,1)}, ...), condition=%wide.region_12.13_spmd.clone, body=%wide.region_9.12_spmd.clone.sunk | while | flops 1581979136 | bytes 88961552 | solution.py:145
  361.7 19.0 %fusion.217 = bf16[4,64,256]{2,1,0:T(8,128)(2,1)} fusion(bf16[2304,4,64]{0,2,1:T(8,128)(2,1)S(1)} %bitcast.245, f32[4,256,2304]{2,1,0:T(8,128)} %fusion.214, f32[4,256,2304]{2,1,0:T(8,128)} %get-tuple-element.631, f32[4,256]{1,0:T(4,128)} %get-tuple-element.632, pred[256,2304]{1,0:T(8,128)(4,1)} %copy-done.5), kind=kOutput, calls=%fused_computation.30.clone.1 | convolution fusion | flops 328011008 | bytes 20779008 | tf_op jit(solution)/shard_map/while/body/eval_jaxpr/mgqk,mkgd->mqgd/dot_general | solution.py:111
  380.7 19.6 %fusion.219 = bf16[4,64,2304]{2,1,0:T(8,128)(2,1)S(1)} fusion(bf16[256,4,64]{0,2,1:T(8,128)(2,1)S(1)} %bitcast.251, f32[4,256,2304]{2,1,0:T(8,128)} %fusion.214, f32[4,256,2304]{2,1,0:T(8,128)} %get-tuple-element.631, f32[4,256]{1,0:T(4,128)} %get-tuple-element.632, pred[256,2304]{1,0:T(8,128)(4,1)} %copy-done.5), kind=kOutput, calls=%fused_computation.27.clone.1 | convolution fusion | flops 328535296 | bytes 20779008 | tf_op jit(solution)/shard_map/while/body/eval_jaxpr/mgqk,mqgd->mkgd/dot_general | solution.py:114
  425.9 19.0 %fusion.217 = bf16[4,64,256]{2,1,0:T(8,128)(2,1)} fusion(bf16[2304,4,64]{0,2,1:T(8,128)(2,1)S(1)} %bitcast.245, f32[4,256,2304]{2,1,0:T(8,128)} %fusion.214, f32[4,256,2304]{2,1,0:T(8,128)} %get-tuple-element.631, f32[4,256]{1,0:T(4,128)} %get-tuple-element.632, pred[256,2304]{1,0:T(8,128)(4,1)} %copy-done.5), kind=kOutput, calls=%fused_computation.30.clone.1 | convolution fusion | flops 328011008 | bytes 20779008 | tf_op jit(solution)/shard_map/while/body/eval_jaxpr/mgqk,mkgd->mqgd/dot_general | solution.py:111
  444.9 19.6 %fusion.219 = bf16[4,64,2304]{2,1,0:T(8,128)(2,1)S(1)} fusion(bf16[256,4,64]{0,2,1:T(8,128)(2,1)S(1)} %bitcast.251, f32[4,256,2304]{2,1,0:T(8,128)} %fusion.214, f32[4,256,2304]{2,1,0:T(8,128)} %get-tuple-element.631, f32[4,256]{1,0:T(4,128)} %get-tuple-element.632, pred[256,2304]{1,0:T(8,128)(4,1)} %copy-done.5), kind=kOutput, calls=%fused_computation.27.clone.1 | convolution fusion | flops 328535296 | bytes 20779008 | tf_op jit(solution)/shard_map/while/body/eval_jaxpr/mgqk,mqgd->mkgd/dot_general | solution.py:114
  490.0 19.0 %fusion.217 = bf16[4,64,256]{2,1,0:T(8,128)(2,1)} fusion(bf16[2304,4,64]{0,2,1:T(8,128)(2,1)S(1)} %bitcast.245, f32[4,256,2304]{2,1,0:T(8,128)} %fusion.214, f32[4,256,2304]{2,1,0:T(8,128)} %get-tuple-element.631, f32[4,256]{1,0:T(4,128)} %get-tuple-element.632, pred[256,2304]{1,0:T(8,128)(4,1)} %copy-done.5), kind=kOutput, calls=%fused_computation.30.clone.1 | convolution fusion | flops 328011008 | bytes 20779008 | tf_op jit(solution)/shard_map/while/body/eval_jaxpr/mgqk,mkgd->mqgd/dot_general | solution.py:111
  509.0 19.6 %fusion.219 = bf16[4,64,2304]{2,1,0:T(8,128)(2,1)S(1)} fusion(bf16[256,4,64]{0,2,1:T(8,128)(2,1)S(1)} %bitcast.251, f32[4,256,2304]{2,1,0:T(8,128)} %fusion.214, f32[4,256,2304]{2,1,0:T(8,128)} %get-tuple-element.631, f32[4,256]{1,0:T(4,128)} %get-tuple-element.632, pred[256,2304]{1,0:T(8,128)(4,1)} %copy-done.5), kind=kOutput, calls=%fused_computation.27.clone.1 | convolution fusion | flops 328535296 | bytes 20779008 | tf_op jit(solution)/shard_map/while/body/eval_jaxpr/mgqk,mqgd->mkgd/dot_general | solution.py:114
  554.1 19.0 %fusion.217 = bf16[4,64,256]{2,1,0:T(8,128)(2,1)} fusion(bf16[2304,4,64]{0,2,1:T(8,128)(2,1)S(1)} %bitcast.245, f32[4,256,2304]{2,1,0:T(8,128)} %fusion.214, f32[4,256,2304]{2,1,0:T(8,128)} %get-tuple-element.631, f32[4,256]{1,0:T(4,128)} %get-tuple-element.632, pred[256,2304]{1,0:T(8,128)(4,1)} %copy-done.5), kind=kOutput, calls=%fused_computation.30.clone.1 | convolution fusion | flops 328011008 | bytes 20779008 | tf_op jit(solution)/shard_map/while/body/eval_jaxpr/mgqk,mkgd->mqgd/dot_general | solution.py:111
  573.1 19.6 %fusion.219 = bf16[4,64,2304]{2,1,0:T(8,128)(2,1)S(1)} fusion(bf16[256,4,64]{0,2,1:T(8,128)(2,1)S(1)} %bitcast.251, f32[4,256,2304]{2,1,0:T(8,128)} %fusion.214, f32[4,256,2304]{2,1,0:T(8,128)} %get-tuple-element.631, f32[4,256]{1,0:T(4,128)} %get-tuple-element.632, pred[256,2304]{1,0:T(8,128)(4,1)} %copy-done.5), kind=kOutput, calls=%fused_computation.27.clone.1 | convolution fusion | flops 328535296 | bytes 20779008 | tf_op jit(solution)/shard_map/while/body/eval_jaxpr/mgqk,mqgd->mkgd/dot_general | solution.py:114
  631.7 13.0 %all-gather = bf16[512,128]{1,0:T(8,128)(2,1)S(1)} all-gather(bf16[64,128]{1,0:T(8,128)(2,1)} %reduce-scatter.2.cloned.1.call-done), channel_id=2, replica_groups=mesh['member'=8,'band'=16] {'member'}, dimensions={0}, use_global_device_ids=true | all-gather | bytes 147456 | tf_op jit(solution)/shard_map/all_gather | solution.py:19
  662.0 17.1 %collective-permute-done.26 = bf16[1,256,1024]{1,2,0:T(8,128)(2,1)S(1)} collective-permute-done((bf16[1,256,1024]{1,2,0:T(8,128)(2,1)}, bf16[1,256,1024]{1,2,0:T(8,128)(2,1)S(1)}, u32[]{:S(2)}, u32[]{:S(2)}) %collective-permute-start.26) | collective-permute-done | bytes 524320 | tf_op jit(solution)/shard_map/ppermute | solution.py:29
  679.1 10.4 %collective-permute-start.24 = (bf16[1,256,1024]{1,2,0:T(8,128)(2,1)S(1)}, bf16[1,256,1024]{1,2,0:T(8,128)(2,1)S(1)}, u32[]{:S(2)}, u32[]{:S(2)}) collective-permute-start(bf16[1,256,1024]{1,2,0:T(8,128)(2,1)S(1)} %copy-done.23), channel_id=1, source_target_pairs={{0,1},{1,2},{2,3},{3,4},{4,5},{5,6},{6,7},{7,8},{8,9},{9,10},{10,1... | collective-permute-start | bytes 1572872 | tf_op jit(solution)/shard_map/ppermute | solution.py:29
  693.6 18.1 %collective-permute-done.24 = bf16[1,256,1024]{1,2,0:T(8,128)(2,1)S(1)} collective-permute-done((bf16[1,256,1024]{1,2,0:T(8,128)(2,1)S(1)}, bf16[1,256,1024]{1,2,0:T(8,128)(2,1)S(1)}, u32[]{:S(2)}, u32[]{:S(2)}) %collective-permute-start.24) | collective-permute-done | bytes 524320 | tf_op jit(solution)/shard_map/ppermute | solution.py:29
  717.7 9.2 %collective-permute-done.22 = bf16[1,256,1024]{1,2,0:T(8,128)(2,1)S(1)} collective-permute-done((bf16[1,256,1024]{1,2,0:T(8,128)(2,1)S(1)}, bf16[1,256,1024]{1,2,0:T(8,128)(2,1)S(1)}, u32[]{:S(2)}, u32[]{:S(2)}) %collective-permute-start.22) | collective-permute-done | bytes 524320 | tf_op jit(solution)/shard_map/ppermute | solution.py:29
  731.8 14.1 %collective-permute-done.20 = bf16[1,256,1024]{1,2,0:T(8,128)(2,1)S(1)} collective-permute-done((bf16[1,256,1024]{1,2,0:T(8,128)(2,1)S(1)}, bf16[1,256,1024]{1,2,0:T(8,128)(2,1)S(1)}, u32[]{:S(2)}, u32[]{:S(2)}) %collective-permute-start.20) | collective-permute-done | bytes 524320 | tf_op jit(solution)/shard_map/ppermute | solution.py:29
  748.1 8.1 %collective-permute-start.30 = (bf16[1,256,1024]{1,2,0:T(8,128)(2,1)S(1)}, bf16[1,256,1024]{1,2,0:T(8,128)(2,1)S(1)}, u32[]{:S(2)}, u32[]{:S(2)}) collective-permute-start(bf16[1,256,1024]{1,2,0:T(8,128)(2,1)S(1)} %copy-done.17), channel_id=1, source_target_pairs={{0,4},{1,5},{2,6},{3,7},{4,8},{5,9},{6,10},{7,11},{8,12},{9,13},{1... | collective-permute-start | bytes 1572872 | tf_op jit(solution)/shard_map/ppermute | solution.py:29
  757.0 10.2 %collective-permute-done.18 = bf16[1,256,1024]{1,2,0:T(8,128)(2,1)S(1)} collective-permute-done((bf16[1,256,1024]{1,2,0:T(8,128)(2,1)S(1)}, bf16[1,256,1024]{1,2,0:T(8,128)(2,1)S(1)}, u32[]{:S(2)}, u32[]{:S(2)}) %collective-permute-start.18) | collective-permute-done | bytes 524320 | tf_op jit(solution)/shard_map/ppermute | solution.py:29
  (326 shorter events, 372.6 us)
Async XLA Ops:
  11.8 115.1 %collective-permute-start.15 = (bf16[1,256,1024]{2,1,0:T(8,128)(2,1)}, bf16[1,256,1024]{2,1,0:T(8,128)(2,1)S(1)}, u32[]{:S(2)}, u32[]{:S(2)}) collective-permute-start(bf16[1,256,1024]{2,1,0:T(8,128)(2,1)} %fusion.73), channel_id=1, source_target_pairs={{4,0},{5,1},{6,2},{7,3},{8,4},{9,5},{10,6},{11,7},{12,8},{13,9},{1... | collective-permute-start | bytes 1572872 | tf_op jit(solution)/shard_map/ppermute | solution.py:29
  13.1 69.9 %collective-permute-start.11 = (bf16[1,256,1024]{2,1,0:T(8,128)(2,1)}, bf16[1,256,1024]{2,1,0:T(8,128)(2,1)}, u32[]{:S(2)}, u32[]{:S(2)}) collective-permute-start(bf16[1,256,1024]{2,1,0:T(8,128)(2,1)} %fusion.73), channel_id=1, source_target_pairs={{0,1},{1,2},{2,3},{3,4},{4,5},{5,6},{6,7},{7,8},{8,9},{9,10},{10,1... | collective-permute-start | bytes 1572872 | tf_op jit(solution)/shard_map/ppermute | solution.py:29
  16.3 62.9 %collective-permute-start.10 = (bf16[1,256,1024]{2,1,0:T(8,128)(2,1)}, bf16[1,256,1024]{2,1,0:T(8,128)(2,1)}, u32[]{:S(2)}, u32[]{:S(2)}) collective-permute-start(bf16[1,256,1024]{2,1,0:T(8,128)(2,1)} %fusion.73), channel_id=1, source_target_pairs={{0,2},{1,3},{2,4},{3,5},{4,6},{5,7},{6,8},{7,9},{8,10},{9,11},{10,... | collective-permute-start | bytes 1572872 | tf_op jit(solution)/shard_map/ppermute | solution.py:29
  20.9 54.5 %collective-permute-start.9 = (bf16[1,256,1024]{2,1,0:T(8,128)(2,1)}, bf16[1,256,1024]{2,1,0:T(8,128)(2,1)}, u32[]{:S(2)}, u32[]{:S(2)}) collective-permute-start(bf16[1,256,1024]{2,1,0:T(8,128)(2,1)} %fusion.73), channel_id=1, source_target_pairs={{0,3},{1,4},{2,5},{3,6},{4,7},{5,8},{6,9},{7,10},{8,11},{9,12},{10... | collective-permute-start | bytes 1572872 | tf_op jit(solution)/shard_map/ppermute | solution.py:29
  25.6 43.5 %collective-permute-start.8 = (bf16[1,256,1024]{2,1,0:T(8,128)(2,1)}, bf16[1,256,1024]{2,1,0:T(8,128)(2,1)}, u32[]{:S(2)}, u32[]{:S(2)}) collective-permute-start(bf16[1,256,1024]{2,1,0:T(8,128)(2,1)} %fusion.73), channel_id=1, source_target_pairs={{0,4},{1,5},{2,6},{3,7},{4,8},{5,9},{6,10},{7,11},{8,12},{9,13},{1... | collective-permute-start | bytes 1572872 | tf_op jit(solution)/shard_map/ppermute | solution.py:29
  79.2 42.1 %collective-permute-start.13 = (bf16[1,256,1024]{2,1,0:T(8,128)(2,1)}, bf16[1,256,1024]{2,1,0:T(8,128)(2,1)S(1)}, u32[]{:S(2)}, u32[]{:S(2)}) collective-permute-start(bf16[1,256,1024]{2,1,0:T(8,128)(2,1)} %fusion.73), channel_id=1, source_target_pairs={{2,0},{3,1},{4,2},{5,3},{6,4},{7,5},{8,6},{9,7},{10,8},{11,9},{12,... | collective-permute-start | bytes 1572872 | tf_op jit(solution)/shard_map/ppermute | solution.py:29
  83.0 41.7 %collective-permute-start.14 = (bf16[1,256,1024]{2,1,0:T(8,128)(2,1)}, bf16[1,256,1024]{2,1,0:T(8,128)(2,1)S(1)}, u32[]{:S(2)}, u32[]{:S(2)}) collective-permute-start(bf16[1,256,1024]{2,1,0:T(8,128)(2,1)} %fusion.73), channel_id=1, source_target_pairs={{3,0},{4,1},{5,2},{6,3},{7,4},{8,5},{9,6},{10,7},{11,8},{12,9},{13... | collective-permute-start | bytes 1572872 | tf_op jit(solution)/shard_map/ppermute | solution.py:29
  88.0 46.4 %collective-permute-start.1 = (bf16[1,256,1024]{2,1,0:T(8,128)(2,1)S(1)}, bf16[1,256,1024]{2,1,0:T(8,128)(2,1)S(1)}, u32[]{:S(2)}, u32[]{:S(2)}) collective-permute-start(bf16[1,256,1024]{2,1,0:T(8,128)(2,1)S(1)} %copy-done.24), channel_id=1, source_target_pairs={{0,3},{1,4},{2,5},{3,6},{4,7},{5,8},{6,9},{7,10},{8,11},{9,12},{10... | collective-permute-start | bytes 1572872 | tf_op jit(solution)/shard_map/ppermute | solution.py:29
  100.3 40.0 %collective-permute-start.2 = (bf16[1,256,1024]{2,1,0:T(8,128)(2,1)S(1)}, bf16[1,256,1024]{2,1,0:T(8,128)(2,1)S(1)}, u32[]{:S(2)}, u32[]{:S(2)}) collective-permute-start(bf16[1,256,1024]{2,1,0:T(8,128)(2,1)S(1)} %copy-done.24), channel_id=1, source_target_pairs={{0,2},{1,3},{2,4},{3,5},{4,6},{5,7},{6,8},{7,9},{8,10},{9,11},{10,... | collective-permute-start | bytes 1572872 | tf_op jit(solution)/shard_map/ppermute | solution.py:29
  124.7 59.8 %collective-permute-start.7 = (bf16[1,256,1024]{2,1,0:T(8,128)(2,1)S(1)}, bf16[1,256,1024]{2,1,0:T(8,128)(2,1)}, u32[]{:S(2)}, u32[]{:S(2)}) collective-permute-start(bf16[1,256,1024]{2,1,0:T(8,128)(2,1)S(1)} %copy-done.24), channel_id=1, source_target_pairs={{4,0},{5,1},{6,2},{7,3},{8,4},{9,5},{10,6},{11,7},{12,8},{13,9},{1... | collective-permute-start | bytes 1572872 | tf_op jit(solution)/shard_map/ppermute | solution.py:29
  134.4 47.4 %collective-permute-start.5 = (bf16[1,256,1024]{2,1,0:T(8,128)(2,1)S(1)}, bf16[1,256,1024]{2,1,0:T(8,128)(2,1)S(1)}, u32[]{:S(2)}, u32[]{:S(2)}) collective-permute-start(bf16[1,256,1024]{2,1,0:T(8,128)(2,1)S(1)} %copy-done.24), channel_id=1, source_target_pairs={{2,0},{3,1},{4,2},{5,3},{6,4},{7,5},{8,6},{9,7},{10,8},{11,9},{12,... | collective-permute-start | bytes 1572872 | tf_op jit(solution)/shard_map/ppermute | solution.py:29
  140.2 42.5 %collective-permute-start.6 = (bf16[1,256,1024]{2,1,0:T(8,128)(2,1)S(1)}, bf16[1,256,1024]{2,1,0:T(8,128)(2,1)}, u32[]{:S(2)}, u32[]{:S(2)}) collective-permute-start(bf16[1,256,1024]{2,1,0:T(8,128)(2,1)S(1)} %copy-done.24), channel_id=1, source_target_pairs={{3,0},{4,1},{5,2},{6,3},{7,4},{8,5},{9,6},{10,7},{11,8},{12,9},{13... | collective-permute-start | bytes 1572872 | tf_op jit(solution)/shard_map/ppermute | solution.py:29
  255.1 76.4 %all-to-all-start.1 = ((bf16[8,32,128]{2,1,0:T(8,128)(2,1)}), bf16[8,32,128]{2,1,0:T(8,128)(2,1)S(1)}, u32[]{:S(2)}, u32[]{:S(2)}) async-start(bf16[8,32,128]{2,1,0:T(8,128)(2,1)} %get-tuple-element.463), calls=%async_computation.1 | async-start | bytes 131072 | tf_op jit(solution)/shard_map/all_to_all | solution.py:243
  260.4 371.3 %reduce-scatter.2.cloned.1.call-start = ((), (), s32[]{:S(2)}) async-start(), calls=%async_computation.3 | async-start | bytes 278528 | tf_op jit(solution)/shard_map/reduce_scatter | solution.py:247
  611.0 34.4 %collective-permute-start.29 = (bf16[1,256,1024]{1,2,0:T(8,128)(2,1)}, bf16[1,256,1024]{1,2,0:T(8,128)(2,1)}, u32[]{:S(2)}, u32[]{:S(2)}) collective-permute-start(bf16[1,256,1024]{1,2,0:T(8,128)(2,1)} %get-tuple-element.455), channel_id=1, source_target_pairs={{0,3},{1,4},{2,5},{3,6},{4,7},{5,8},{6,9},{7,10},{8,11},{9,12},{10... | collective-permute-start | bytes 1572872 | tf_op jit(solution)/shard_map/ppermute | solution.py:29
  621.1 146.9 %collective-permute-start.17 = (bf16[1,256,1024]{1,2,0:T(8,128)(2,1)}, bf16[1,256,1024]{1,2,0:T(8,128)(2,1)}, u32[]{:S(2)}, u32[]{:S(2)}) collective-permute-start(bf16[1,256,1024]{1,2,0:T(8,128)(2,1)} %get-tuple-element.454), channel_id=1, source_target_pairs={{4,0},{5,1},{6,2},{7,3},{8,4},{9,5},{10,6},{11,7},{12,8},{13,9},{1... | collective-permute-start | bytes 1572872 | tf_op jit(solution)/shard_map/ppermute | solution.py:29
  622.4 35.7 %collective-permute-start.27 = (bf16[1,256,1024]{1,2,0:T(8,128)(2,1)}, bf16[1,256,1024]{1,2,0:T(8,128)(2,1)}, u32[]{:S(2)}, u32[]{:S(2)}) collective-permute-start(bf16[1,256,1024]{1,2,0:T(8,128)(2,1)} %get-tuple-element.456), channel_id=1, source_target_pairs={{0,2},{1,3},{2,4},{3,5},{4,6},{5,7},{6,8},{7,9},{8,10},{9,11},{10,... | collective-permute-start | bytes 1572872 | tf_op jit(solution)/shard_map/ppermute | solution.py:29
  627.2 63.2 %collective-permute-start.25 = (bf16[1,256,1024]{1,2,0:T(8,128)(2,1)}, bf16[1,256,1024]{1,2,0:T(8,128)(2,1)}, u32[]{:S(2)}, u32[]{:S(2)}) collective-permute-start(bf16[1,256,1024]{1,2,0:T(8,128)(2,1)} %get-tuple-element.457), channel_id=1, source_target_pairs={{0,1},{1,2},{2,3},{3,4},{4,5},{5,6},{6,7},{7,8},{8,9},{9,10},{10,1... | collective-permute-start | bytes 1572872 | tf_op jit(solution)/shard_map/ppermute | solution.py:29
  645.4 69.1 %collective-permute-start.23 = (bf16[1,256,1024]{1,2,0:T(8,128)(2,1)}, bf16[1,256,1024]{1,2,0:T(8,128)(2,1)S(1)}, u32[]{:S(2)}, u32[]{:S(2)}) collective-permute-start(bf16[1,256,1024]{1,2,0:T(8,128)(2,1)} %get-tuple-element.458), channel_id=1, source_target_pairs={{1,0},{2,1},{3,2},{4,3},{5,4},{6,5},{7,6},{8,7},{9,8},{10,9},{11,1... | collective-permute-start | bytes 1572872 | tf_op jit(solution)/shard_map/ppermute | solution.py:29
  658.1 71.5 %collective-permute-start.21 = (bf16[1,256,1024]{1,2,0:T(8,128)(2,1)S(1)}, bf16[1,256,1024]{1,2,0:T(8,128)(2,1)S(1)}, u32[]{:S(2)}, u32[]{:S(2)}) collective-permute-start(bf16[1,256,1024]{1,2,0:T(8,128)(2,1)S(1)} %copy-done.20), channel_id=1, source_target_pairs={{2,0},{3,1},{4,2},{5,3},{6,4},{7,5},{8,6},{9,7},{10,8},{11,9},{12,... | collective-permute-start | bytes 1572872 | tf_op jit(solution)/shard_map/ppermute | solution.py:29
  679.1 32.6 %collective-permute-start.24 = (bf16[1,256,1024]{1,2,0:T(8,128)(2,1)S(1)}, bf16[1,256,1024]{1,2,0:T(8,128)(2,1)S(1)}, u32[]{:S(2)}, u32[]{:S(2)}) collective-permute-start(bf16[1,256,1024]{1,2,0:T(8,128)(2,1)S(1)} %copy-done.23), channel_id=1, source_target_pairs={{0,1},{1,2},{2,3},{3,4},{4,5},{5,6},{6,7},{7,8},{8,9},{9,10},{10,1... | collective-permute-start | bytes 1572872 | tf_op jit(solution)/shard_map/ppermute | solution.py:29
  690.4 57.7 %collective-permute-start.19 = (bf16[1,256,1024]{1,2,0:T(8,128)(2,1)S(1)}, bf16[1,256,1024]{1,2,0:T(8,128)(2,1)S(1)}, u32[]{:S(2)}, u32[]{:S(2)}) collective-permute-start(bf16[1,256,1024]{1,2,0:T(8,128)(2,1)S(1)} %copy-done.18), channel_id=1, source_target_pairs={{3,0},{4,1},{5,2},{6,3},{7,4},{8,5},{9,6},{10,7},{11,8},{12,9},{13... | collective-permute-start | bytes 1572872 | tf_op jit(solution)/shard_map/ppermute | solution.py:29
  714.5 55.3 %collective-permute-start.31 = (bf16[1,256,1024]{1,2,0:T(8,128)(2,1)S(1)}, bf16[1,256,1024]{1,2,0:T(8,128)(2,1)S(1)}, u32[]{:S(2)}, u32[]{:S(2)}) collective-permute-start(bf16[1,256,1024]{1,2,0:T(8,128)(2,1)S(1)} %copy-done.15), channel_id=1, source_target_pairs={{0,4},{1,5},{2,6},{3,7},{4,8},{5,9},{6,10},{7,11},{8,12},{9,13},{1... | collective-permute-start | bytes 1572872 | tf_op jit(solution)/shard_map/ppermute | solution.py:29
  729.6 41.8 %collective-permute-start.16 = (bf16[1,256,1024]{1,2,0:T(8,128)(2,1)S(1)}, bf16[1,256,1024]{1,2,0:T(8,128)(2,1)S(1)}, u32[]{:S(2)}, u32[]{:S(2)}) collective-permute-start(bf16[1,256,1024]{1,2,0:T(8,128)(2,1)S(1)} %copy-done.16), channel_id=1, source_target_pairs={{4,0},{5,1},{6,2},{7,3},{8,4},{9,5},{10,6},{11,7},{12,8},{13,9},{1... | collective-permute-start | bytes 1572872 | tf_op jit(solution)/shard_map/ppermute | solution.py:29
  (56 other events, 1014.1 us)
Sparse Core Ops, SparseCore 0:
  335.4 72.1 reduce-scatter.1
